TPU v7x, 32 devices: a whole 2x2x4 slice. The times are simulated.
32 devices in a mesh: group: 2 (over x), col: 16 (over z, y, core).
Axes of the slice: x: 2, y: 2, z: 4, core: 2. Of those that a mesh axis runs over, the one named last changes fastest.
Arguments:
- homolog_embedding: bfloat16 [192, 64, 256], P('group', 'col'), parts along dimension 0, may hold values from -6 to 6
- left_factor_matrix: bfloat16 [256, 32], replicated, may hold values from -0.375 to 0.375
- right_factor_matrix: bfloat16 [256, 32], replicated, may hold values from -0.375 to 0.375
- decoder: bfloat16 [1024, 128], replicated, may hold values from -2 to 2
- pair_output_bias: float32 [128], replicated, may hold values from -3 to 3
- pair_output_gradient: bfloat16 [128, 64, 128], P('group', 'col'), parts along dimension 0, may hold values from -6 to 6
Outputs:
- first_operand_gradient: float32 [192, 64, 32], P('group', 'col'), parts along dimension 0
- second_operand_gradient: float32 [192, 64, 32], P('group', 'col'), parts along dimension 0
- alignment_gradient: bfloat16 [192, 64, 256], P('group', 'col'), parts along dimension 0
There are 2 independent parts, one for each index of `group`. A program takes and returns all parts, laid end to end along the dimension named above; an argument that names none is the same for every part. Nothing has to cross between parts.
All inputs are finite; a program needn't handle non-finite values.
Results may differ from a plain program's by a relative error of at most 0.0083.
Values may be sent and summed in bfloat16 or wider, within the bound.
A program may use at most 64 MiB of HBM per device.

v0:
```python
import jax
import jax.numpy as jnp
from jax import lax
from jax.sharding import PartitionSpec as P


def per_device(
    homolog_embedding,
    left_factor_matrix,
    right_factor_matrix,
    decoder,
    pair_output_bias,
    pair_output_gradient,
):
    alignment_row_count, local_residue_start, alignment_channel_width = homolog_embedding.shape
    operand_channel_width = left_factor_matrix.shape[1]
    channels = decoder.shape[1]
    residue_total_count = local_residue_start * lax.axis_size("col")
    reciprocal_rows = 1.0 / alignment_row_count
    block_res = local_residue_start * max(1, 96 // local_residue_start)
    alignment_flattened_rows = homolog_embedding.reshape(
        alignment_row_count * local_residue_start, alignment_channel_width
    )
    first_operand_rows = (
        jnp.dot(alignment_flattened_rows, left_factor_matrix, preferred_element_type=jnp.float32)
        .astype(jnp.bfloat16)
        .reshape(alignment_row_count, local_residue_start * operand_channel_width)
    )
    second_operand_rows = (
        jnp.dot(alignment_flattened_rows, right_factor_matrix, preferred_element_type=jnp.float32)
        .astype(jnp.bfloat16)
        .reshape(alignment_row_count, local_residue_start * operand_channel_width)
    )
    second_operand_local = second_operand_rows.reshape(
        alignment_row_count, local_residue_start, operand_channel_width
    )

    def outer_slopes(slope_rows, rows_by_length, col_span):
        backward = (
            jnp.dot(slope_rows, decoder.T, preferred_element_type=jnp.float32) * reciprocal_rows
        )
        return backward.astype(jnp.bfloat16).reshape(
            rows_by_length, col_span, operand_channel_width, operand_channel_width
        )

    offset_col = jnp.int32(0)
    second_operand_gradient = jnp.zeros(
        (alignment_row_count, local_residue_start, operand_channel_width), jnp.float32
    )
    stored = jnp.zeros((residue_total_count, local_residue_start * channels), jnp.bfloat16)
    left_segment = lax.all_gather(first_operand_rows, "col", axis=1, tiled=True)
    right_segment = lax.all_gather(second_operand_rows, "col", axis=1, tiled=True)
    right_whole = right_segment
    piece_res = left_segment.shape[1] // operand_channel_width
    first_res = offset_col // operand_channel_width
    collected = []
    for split_offset in range(0, piece_res, block_res):
        split_rows_by_length = min(block_res, piece_res - split_offset)
        split_left_block = left_segment[
            :,
            split_offset
            * operand_channel_width : (split_offset + split_rows_by_length)
            * operand_channel_width,
        ].reshape(alignment_row_count, split_rows_by_length, operand_channel_width)
        collected.append((split_rows_by_length, split_left_block, first_res + split_offset))
    for rows_by_length, left_block, first_row in collected:
        products = (
            jnp.einsum(
                "sic,sjd->ijcd",
                left_block,
                second_operand_local,
                preferred_element_type=jnp.float32,
            )
            * reciprocal_rows
        )
        products = products.astype(jnp.bfloat16).reshape(
            rows_by_length * local_residue_start, operand_channel_width * operand_channel_width
        )
        linear = jnp.dot(products, decoder, preferred_element_type=jnp.float32) + pair_output_bias
        upstream = lax.dynamic_slice_in_dim(pair_output_gradient, first_row, rows_by_length, 0)
        upstream = upstream.reshape(rows_by_length * local_residue_start, channels).astype(
            jnp.float32
        )
        accumulate_slope_rows = (upstream * 2.0 * jnp.maximum(linear, 0.0)).astype(jnp.bfloat16)
        stored = lax.dynamic_update_slice_in_dim(
            stored,
            accumulate_slope_rows.reshape(rows_by_length, local_residue_start * channels),
            first_row,
            0,
        )
        accumulate_slopes = outer_slopes(accumulate_slope_rows, rows_by_length, local_residue_start)
        second_operand_gradient = second_operand_gradient + jnp.einsum(
            "ijcd,sic->sjd", accumulate_slopes, left_block, preferred_element_type=jnp.float32
        )
    second_operand_gradient, stored, right_whole = (second_operand_gradient, stored, right_whole)
    received = lax.all_to_all(stored, "col", split_axis=0, concat_axis=1, tiled=True)
    right_all = right_whole.reshape(alignment_row_count, residue_total_count, operand_channel_width)
    col_span = local_residue_start * max(
        max(1, 96 // local_residue_start), lax.axis_size("col") // 8
    )
    first_operand_gradient = jnp.zeros(
        (alignment_row_count, local_residue_start, operand_channel_width), jnp.float32
    )
    for offset in range(0, residue_total_count, col_span):
        width_cols = min(col_span, residue_total_count - offset)
        slope_rows = received[:, offset * channels : (offset + width_cols) * channels].reshape(
            local_residue_start * width_cols, channels
        )
        slopes = outer_slopes(slope_rows, local_residue_start, width_cols)
        first_operand_gradient = first_operand_gradient + jnp.einsum(
            "ijcd,sjd->sic",
            slopes,
            right_all[:, offset : offset + width_cols],
            preferred_element_type=jnp.float32,
        )
    first_operand_gradient_step = first_operand_gradient.astype(jnp.bfloat16).reshape(
        alignment_row_count * local_residue_start, operand_channel_width
    )
    second_operand_gradient_step = second_operand_gradient.astype(jnp.bfloat16).reshape(
        alignment_row_count * local_residue_start, operand_channel_width
    )
    alignment_gradient = jnp.dot(
        first_operand_gradient_step, left_factor_matrix.T, preferred_element_type=jnp.float32
    ) + jnp.dot(
        second_operand_gradient_step, right_factor_matrix.T, preferred_element_type=jnp.float32
    )
    alignment_gradient = alignment_gradient.astype(jnp.bfloat16).reshape(
        alignment_row_count, local_residue_start, alignment_channel_width
    )
    return (first_operand_gradient, second_operand_gradient, alignment_gradient)


def solution(mesh):
    placed = (P("group", "col", None), P(), P(), P(), P(), P("group", "col", None))
    return jax.shard_map(
        per_device,
        mesh=mesh,
        in_specs=placed,
        out_specs=(P("group", "col", None), P("group", "col", None), P("group", "col", None)),
        check_vma=False,
    )
```

profile of v0, /device:TPU:0, one launch (start us, length us, event | category | flops | bytes accessed | tf_op | source)
XLA Modules:
  0.0 74.2 jit_solution(9161705522396213601)
XLA Ops:
  0.6 0.0 copy-start
  0.6 0.0 copy-start.3
  0.7 1.0 %reshape.53 = bf16[384,256]{1,0:T(8,128)(2,1)S(1)} reshape(bf16[96,4,256]{2,1,0:T(4,128)(2,1)} %param.6) | data formatting | bytes 393216 | tf_op jit(solution)/shard_map/reshape | solution.py:21
  1.7 0.9 %convolution_convert_fusion = bf16[384,32]{0,1:T(8,128)(2,1)S(1)} fusion(bf16[384,256]{1,0:T(8,128)(2,1)S(1)} %reshape.53, bf16[256,32]{0,1:T(8,128)(2,1)} %param.7), kind=kOutput, calls=%fused_computation.14 | convolution fusion | flops 6303744 | bytes 237568 | tf_op jit(solution)/shard_map/dot_general | solution.py:25
  2.6 0.1 copy.31
  2.7 0.1 reshape.56
  2.8 24.2 %all_gather.7 = bf16[96,2048]{1,0:T(8,128)(2,1)S(1)} all-gather(bf16[96,128]{1,0:T(8,128)(2,1)S(1)} %reshape.56), channel_id=1, replica_groups=mesh['group'=2,'col'=16] {'col'}, dimensions={1}, use_global_device_ids=true | all-gather | bytes 417792 | tf_op jit(solution)/shard_map/all_gather | solution.py:51
  27.0 0.3 copy.32
  27.3 0.0 copy-done.3
  27.3 0.2 convolution_convert_fusion.1
  27.5 0.1 copy.28
  27.6 1.6 %fusion = bf16[64,4,32,32]{0,3,2,1:T(8,128)(2,1)} fusion(bf16[96,64,32]{0,2,1:T(8,128)(2,1)S(1)} %bitcast.48, bf16[96,4,32,1]{2,1,0,3:T(4,128)(2,1)S(1)} %bitcast.51), kind=kOutput, calls=%fused_computation.1 | convolution fusion | flops 50855936 | bytes 942080 | tf_op jit(solution)/shard_map/sic,sjd->ijcd/dot_general | solution.py:68
  29.3 4.2 %copy.35 = bf16[64,4,32,32]{3,2,1,0:T(8,128)(2,1)S(1)} copy(bf16[64,4,32,32]{0,3,2,1:T(8,128)(2,1)} %fusion) | data formatting | bytes 1048576 | tf_op jit(solution)/shard_map/convert_element_type | solution.py:76
  33.5 0.0 copy-start.4
  33.5 2.2 %reshape.58 = bf16[256,1024]{1,0:T(8,128)(2,1)S(1)} reshape(bf16[64,4,32,32]{3,2,1,0:T(8,128)(2,1)S(1)} %copy.35) | data formatting | bytes 1048576 | tf_op jit(solution)/shard_map/reshape | solution.py:76
  35.7 0.9 %convert_multiply_fusion = f32[64,4,128]{2,1,0:T(4,128)S(1)} fusion(bf16[64,4,128]{2,1,0:T(4,128)(2,1)} %param.11), kind=kLoop, calls=%fused_computation.18 | loop fusion | flops 65536 | bytes 196608 | tf_op jit(solution)/shard_map/mul | solution.py:84
  36.6 0.0 copy-done
  36.6 0.0 copy-done.4
  36.6 0.3 fusion.6
  36.9 0.7 all_to_all.12
  37.6 4.2 %all-to-all-start = ((bf16[16,4,512]{2,1,0:T(4,128)(2,1)}), bf16[16,4,512]{2,1,0:T(4,128)(2,1)}, u32[]{:S(2)}, u32[]{:S(2)}) async-start(bf16[16,4,512]{2,1,0:T(4,128)(2,1)} %all_to_all.12), calls=%async_computation | async-start | bytes 131072 | tf_op jit(solution)/shard_map/all_to_all | solution.py:96
  41.7 0.7 reshape.54
  42.5 0.3 fusion.2
  42.8 0.0 copy-start.1
  42.8 1.6 %reshape.61 = bf16[64,4,32,32]{3,2,1,0:T(8,128)(2,1)S(1)} reshape(bf16[256,1024]{1,0:T(8,128)(2,1)S(1)} %fusion.2) | data formatting | bytes 1048576 | tf_op jit(solution)/shard_map/reshape | solution.py:42
  44.4 1.3 %fusion.11 = (bf16[96,4,32]{0,2,1:T(8,128)(2,1)S(1)}, f32[96,4,32]{0,2,1:T(8,128)}) fusion(bf16[96,64,32,1]{0,2,3,1:T(8,128)(2,1)S(1)} %bitcast.49, bf16[64,4,32,32]{3,2,1,0:T(8,128)(2,1)S(1)} %reshape.61), kind=kOutput, calls=%fused_computation.21 | convolution fusion | flops 50343936 | bytes 991232 | tf_op jit(solution)/shard_map/ijcd,sic->sjd/dot_general | solution.py:92
  45.7 0.0 copy-done.1
  45.7 22.7 %all_gather.6 = bf16[96,2048]{1,0:T(8,128)(2,1)S(1)} all-gather(bf16[96,128]{1,0:T(8,128)(2,1)S(1)} %copy-done.1), channel_id=1, replica_groups=mesh['group'=2,'col'=16] {'col'}, dimensions={1}, use_global_device_ids=true | all-gather | bytes 417792 | tf_op jit(solution)/shard_map/all_gather | solution.py:52
  68.4 0.3 copy.29
  68.7 0.1 copy.41
  68.8 0.0 all-to-all-done
  68.8 0.9 %copy.36 = bf16[4,16,512]{2,1,0:T(8,128)(2,1)S(1)} copy(bf16[4,16,512]{2,0,1:T(4,128)(2,1)} %bitcast.8) | data formatting | bytes 131072 | tf_op jit(solution)/shard_map/all_to_all | solution.py:96
  69.7 0.1 reshape.59
  69.7 0.3 fusion.1
  70.0 0.0 copy-start.2
  70.0 1.6 %reshape.71 = bf16[4,64,32,32]{3,2,1,0:T(8,128)(2,1)S(1)} reshape(bf16[256,1024]{1,0:T(8,128)(2,1)S(1)} %fusion.1) | data formatting | bytes 1048576 | tf_op jit(solution)/shard_map/reshape | solution.py:42
  71.6 1.3 %fusion.10 = (bf16[96,4,32]{0,2,1:T(8,128)(2,1)S(1)}, f32[96,4,32]{0,2,1:T(8,128)}) fusion(bf16[96,64,32,1]{0,2,1,3:T(8,128)(2,1)S(1)} %bitcast.50, bf16[4,64,32,32]{3,2,1,0:T(8,128)(2,1)S(1)} %reshape.71), kind=kOutput, calls=%fused_computation.20 | convolution fusion | flops 50343936 | bytes 991232 | tf_op jit(solution)/shard_map/ijcd,sjd->sic/dot_general | solution.py:110
  73.0 0.1 copy.40
  73.1 0.0 copy-done.2
  73.1 0.2 fusion.12
  73.3 0.2 fusion.3
  73.5 0.7 reshape.64
Async XLA Ops:
  0.6 36.0 %copy-start = (bf16[1024,128]{1,0:T(8,128)(2,1)S(1)}, bf16[1024,128]{1,0:T(8,128)(2,1)}, u32[]{:S(2)}) copy-start(bf16[1024,128]{1,0:T(8,128)(2,1)} %param.9) | copy-start | bytes 786436
  0.6 26.7 %copy-start.3 = (bf16[256,32]{0,1:T(8,128)(2,1)S(1)}, bf16[256,32]{0,1:T(8,128)(2,1)}, u32[]{:S(2)}) copy-start(bf16[256,32]{0,1:T(8,128)(2,1)} %param.8) | copy-start | bytes 49156
  33.5 3.1 %copy-start.4 = (f32[128]{0:T(128)S(1)}, f32[128]{0:T(128)}, u32[]{:S(2)}) copy-start(f32[128]{0:T(128)} %param.10) | copy-start | bytes 1540
  37.6 31.2 %all-to-all-start = ((bf16[16,4,512]{2,1,0:T(4,128)(2,1)}), bf16[16,4,512]{2,1,0:T(4,128)(2,1)}, u32[]{:S(2)}, u32[]{:S(2)}) async-start(bf16[16,4,512]{2,1,0:T(4,128)(2,1)} %all_to_all.12), calls=%async_computation | async-start | bytes 131072 | tf_op jit(solution)/shard_map/all_to_all | solution.py:96
  42.8 3.0 %copy-start.1 = (bf16[96,128]{1,0:T(8,128)(2,1)S(1)}, bf16[96,128]{1,0:T(8,128)(2,1)}, u32[]{:S(2)}) copy-start(bf16[96,128]{1,0:T(8,128)(2,1)} %reshape.54) | copy-start | bytes 73732
  70.0 3.1 %copy-start.2 = (bf16[256,32]{0,1:T(8,128)(2,1)S(1)}, bf16[256,32]{0,1:T(8,128)(2,1)}, u32[]{:S(2)}) copy-start(bf16[256,32]{0,1:T(8,128)(2,1)} %param.7) | copy-start | bytes 49156
where the time goes:
time: 74.6 us; the launch traced here: 74.2 us
  blocking collectives  46.9 us (63%)
  local copies, waits for them, and re-layouts  14.9 us (20%)
  matrix products  6.57 us (9%)
  starting transfers between devices  4.16 us (6%)
  other arithmetic  0.87 us (1%)
  between operations  0.86 us (1%)
    all_gather x1, blocking collectives, per_device(): left_segment = lax.all_gather(first_operand_rows, 'col', axis=1, tiled=True)  24.2 us
    all_gather x1, blocking collectives, per_device(): lax.all_gather(second_operand_rows, 'col', axis=1, tiled=True)  22.7 us
    convert_element_type x1, local copies, waits for them, and re-layouts, per_device(): products.astype(jnp.bfloat16)  4.19 us
    all_to_all x1, starting transfers between devices, per_device(): lax.all_to_all(stored, 'col', split_axis=0, concat_axis=1, tiled=True)  4.16 us
    reshape x2, local copies, waits for them, and re-layouts, outer_slopes(): backward.astype(jnp.bfloat16)  3.16 us
    reshape x1, local copies, waits for them, and re-layouts, per_device(): products.astype(jnp.bfloat16)  2.23 us
    dot_general x1, matrix products, per_device(): jnp.einsum('sic,sjd->ijcd', left_block, second_operand_local, preferred_e...  1.63 us
    all_to_all x2, local copies, waits for them, and re-layouts, per_device(): lax.all_to_all(stored, 'col', split_axis=0, concat_axis=1, tiled=True)  1.52 us
  transfers between devices with their start and end apart: 1, of which 0 were waited for; matrix products, arithmetic and copies ran while one was open for 6% of the time, Pallas kernels for 0%

commit v1 on v0

v1 whole, which is shorter than its diff:
```python
import functools

import jax
import jax.numpy as jnp
from jax import lax
from jax.experimental import pallas as pl
from jax.experimental.pallas import tpu as pltpu
from jax.sharding import PartitionSpec as P

MESH = pl.DeviceIdType.MESH
F32 = jnp.float32
BF16 = jnp.bfloat16


def dot(x, y, dims=((1,), (0,))):
    return lax.dot_general(x, y, (dims, ((), ())), preferred_element_type=F32)


NT = ((1,), (1,))
TN = ((0,), (0,))


def kernel(
    inner,
    outer,
    e_ref,
    wl_ref,
    wr_ref,
    dec_ref,
    bias_ref,
    g_ref,
    first_ref,
    second_ref,
    align_ref,
    lbuf,
    rbuf,
    gbuf,
    fown,
    sown,
    fsend,
    ssend,
    fbuf,
    sbuf,
    wpad,
    bd,
    perm,
    gf,
    mt,
    s2,
    l_ss,
    l_rs,
    r_ss,
    r_rs,
    g_ss,
    g_rs,
    f_ss,
    f_rs,
    s_ss,
    s_rs,
    own_sem,
):
    rows, res, width = e_ref.shape
    fac = wl_ref.shape[0]
    chan = dec_ref.shape[1]
    blk = res * fac
    ni = outer * res
    recip = 1.0 / rows
    me = lax.axis_index("col")
    a = lax.rem(me, inner)
    b = me // inner

    inner_peers = [lax.rem(a + k, inner) for k in range(1, inner)]
    outer_peers = [lax.rem(b + k, outer) for k in range(1, outer)]

    def inner_dev(p):
        return {"col": b * inner + p}

    def outer_dev(p):
        return {"col": p * inner + a}

    barrier = pltpu.get_barrier_semaphore()
    for p in outer_peers:
        pl.semaphore_signal(barrier, inc=1, device_id=outer_dev(p), device_id_type=MESH)
    for p in inner_peers:
        pl.semaphore_signal(barrier, inc=1, device_id=inner_dev(p), device_id_type=MESH)

    own_g = pltpu.make_async_copy(g_ref.at[:, pl.ds(a * res, res)], gbuf.at[a], own_sem)
    own_g.start()

    wpad[...] = jnp.zeros_like(wpad)
    for r in range(res):
        wpad[r, r * fac : (r + 1) * fac, :] = wl_ref[...]
        wpad[r, blk + r * fac : blk + (r + 1) * fac, :] = wr_ref[...]
    acc = dot(e_ref[:, 0, :], wpad[0], NT)
    for r in range(1, res):
        acc = acc + dot(e_ref[:, r, :], wpad[r], NT)
    acc = acc.astype(BF16)
    lbuf[b] = acc[:, :blk]
    rbuf[a] = acc[:, blk:]

    pl.semaphore_wait(barrier, inner + outer - 2)

    def send(src, dst, ss, rs, dev):
        c = pltpu.make_async_remote_copy(
            src_ref=src, dst_ref=dst, send_sem=ss, recv_sem=rs, device_id=dev, device_id_type=MESH
        )
        c.start()
        return c

    sends = []
    for k, p in enumerate(outer_peers):
        sends.append(send(lbuf.at[b], lbuf.at[b], l_ss.at[k], l_rs.at[b], outer_dev(p)))
    for k, p in enumerate(inner_peers):
        sends.append(send(rbuf.at[a], rbuf.at[a], r_ss.at[k], r_rs.at[a], inner_dev(p)))
    for k, p in enumerate(inner_peers):
        sends.append(
            send(
                g_ref.at[:, pl.ds(p * res, res)], gbuf.at[a], g_ss.at[k], g_rs.at[a], inner_dev(p)
            )
        )

    def arrive(buf, rs, p, dev):
        pltpu.make_async_remote_copy(
            src_ref=buf.at[p],
            dst_ref=buf.at[p],
            send_sem=rs.at[p],
            recv_sem=rs.at[p],
            device_id=dev,
            device_id_type=MESH,
        ).wait_recv()

    bd[...] = jnp.zeros_like(bd)
    for c in range(fac):
        piece = dec_ref[c * fac : (c + 1) * fac, :]
        for r in range(res):
            bd[c * blk + r * fac : c * blk + (r + 1) * fac, r * chan : (r + 1) * chan] = piece
    out_pos = lax.broadcasted_iota(jnp.int32, perm.shape, 0)
    in_pos = lax.broadcasted_iota(jnp.int32, perm.shape, 1)
    hit = in_pos == lax.rem(out_pos, ni) * fac + out_pos // ni
    perm[...] = jnp.where(hit, 1.0, 0.0).astype(BF16)

    own_g.wait()
    for p in outer_peers:
        arrive(lbuf, l_rs, p, outer_dev(p))
    left = jnp.concatenate([lbuf[q] for q in range(outer)], axis=1)
    left_p = dot(left, perm[...], NT).astype(BF16)

    for p in inner_peers:
        arrive(rbuf, r_rs, p, inner_dev(p))
    right = jnp.concatenate([rbuf[q] for q in range(inner)], axis=1)
    prod = (dot(left_p, right, TN) * recip).astype(BF16)
    for c in range(fac):
        for q in range(inner):
            mt[q * ni : (q + 1) * ni, c * blk : (c + 1) * blk] = prod[
                c * ni : (c + 1) * ni, q * blk : (q + 1) * blk
            ]
    for p in inner_peers:
        arrive(gbuf, g_rs, p, inner_dev(p))
    for q in range(inner):
        up = gbuf[q].reshape(ni, res, chan).astype(F32)
        for r in range(res):
            gf[q * ni : (q + 1) * ni, r * chan : (r + 1) * chan] = up[:, r, :]
    bias = jnp.concatenate([bias_ref[...]] * res, axis=1)
    linear = dot(mt[...], bd[...]) + bias
    pre = (gf[...] * 2.0 * jnp.maximum(linear, 0.0)).astype(BF16)
    slopes = (dot(pre, bd[...], NT) * recip).astype(BF16)
    for c in range(fac):
        for q in range(inner):
            s2[c * ni : (c + 1) * ni, q * blk : (q + 1) * blk] = slopes[
                q * ni : (q + 1) * ni, c * blk : (c + 1) * blk
            ]

    first_part = dot(right, s2[...], NT).astype(BF16)
    first_part = dot(first_part, perm[...])
    for q in range(outer):
        term = first_part[:, q * blk : (q + 1) * blk]
        fown[q] = term
        fsend[q] = term.astype(BF16)
    for k, p in enumerate(outer_peers):
        sends.append(send(fsend.at[p], fbuf.at[b], f_ss.at[k], f_rs.at[b], outer_dev(p)))
    second_part = dot(left_p, s2[...])
    for q in range(inner):
        term = second_part[:, q * blk : (q + 1) * blk]
        sown[q] = term
        ssend[q] = term.astype(BF16)
    for k, p in enumerate(inner_peers):
        sends.append(send(ssend.at[p], sbuf.at[a], s_ss.at[k], s_rs.at[a], inner_dev(p)))

    second = sown[a]
    for p in inner_peers:
        arrive(sbuf, s_rs, p, inner_dev(p))
        second = second + sbuf[p].astype(F32)
    second_ref[...] = second.T
    first = fown[b]
    for p in outer_peers:
        arrive(fbuf, f_rs, p, outer_dev(p))
        first = first + fbuf[p].astype(F32)
    first_ref[...] = first.T
    both = jnp.concatenate([first, second], axis=1).astype(BF16)
    for r in range(res):
        align_ref[:, r, :] = dot(both, wpad[r]).astype(BF16)
    for c in sends:
        c.wait_send()


def per_device(
    homolog_embedding,
    left_factor_matrix,
    right_factor_matrix,
    decoder,
    pair_output_bias,
    pair_output_gradient,
):
    rows, res, width = homolog_embedding.shape
    fac = left_factor_matrix.shape[1]
    chan = decoder.shape[1]
    count = lax.axis_size("col")
    inner = max(d for d in range(1, count + 1) if count % d == 0 and d * d <= count)
    outer = count // inner
    blk = res * fac
    ni = outer * res
    dma = pltpu.SemaphoreType.DMA
    first, second, align = pl.pallas_call(
        functools.partial(kernel, inner, outer),
        out_shape=[
            jax.ShapeDtypeStruct((blk, rows), F32),
            jax.ShapeDtypeStruct((blk, rows), F32),
            jax.ShapeDtypeStruct((rows, res, width), BF16),
        ],
        in_specs=[pl.BlockSpec(memory_space=pltpu.VMEM)] * 6,
        out_specs=[pl.BlockSpec(memory_space=pltpu.VMEM)] * 3,
        scratch_shapes=[
            pltpu.VMEM((outer, rows, blk), BF16),
            pltpu.VMEM((inner, rows, blk), BF16),
            pltpu.VMEM((inner, outer, res, res, chan), BF16),
            pltpu.VMEM((outer, rows, blk), F32),
            pltpu.VMEM((inner, rows, blk), F32),
            pltpu.VMEM((outer, rows, blk), BF16),
            pltpu.VMEM((inner, rows, blk), BF16),
            pltpu.VMEM((outer, rows, blk), BF16),
            pltpu.VMEM((inner, rows, blk), BF16),
            pltpu.VMEM((res, 2 * blk, width), BF16),
            pltpu.VMEM((fac * blk, res * chan), BF16),
            pltpu.VMEM((fac * ni, fac * ni), BF16),
            pltpu.VMEM((inner * ni, res * chan), F32),
            pltpu.VMEM((inner * ni, fac * blk), BF16),
            pltpu.VMEM((fac * ni, inner * blk), BF16),
            dma((outer,)),
            dma((outer,)),
            dma((inner,)),
            dma((inner,)),
            dma((inner,)),
            dma((inner,)),
            dma((outer,)),
            dma((outer,)),
            dma((inner,)),
            dma((inner,)),
            dma,
        ],
        compiler_params=pltpu.CompilerParams(collective_id=0, has_side_effects=True),
        name="pair_backward",
    )(
        homolog_embedding,
        left_factor_matrix.T,
        right_factor_matrix.T,
        decoder,
        pair_output_bias.reshape(1, chan),
        pair_output_gradient.reshape(outer, inner * res, res, chan),
    )
    first = first.reshape(res, fac, rows).transpose(2, 0, 1)
    second = second.reshape(res, fac, rows).transpose(2, 0, 1)
    return first, second, align


def solution(mesh):
    placed = (P("group", "col", None), P(), P(), P(), P(), P("group", "col", None))
    return jax.shard_map(
        per_device,
        mesh=mesh,
        in_specs=placed,
        out_specs=(P("group", "col", None), P("group", "col", None), P("group", "col", None)),
        check_vma=False,
    )
```

time: 74.6 us -> 23.5 us (0.32)
  blocking collectives: 46.9 us -> 0 us
  Pallas kernels: 0 us -> 18.9 us
  local copies, waits for them, and re-layouts: 14.9 us -> 3.67 us
  matrix products: 6.57 us -> 0 us
  starting transfers between devices: 4.16 us -> 0 us
  other arithmetic: 0.87 us -> 0 us
    all_gather x2 -> x0, blocking collectives: 46.9 us -> none  [the longest x1 24.2 us: per_device(): left_segment = lax.all_gather(first_operand_rows, 'col', axis=1, tiled=True)]
    pallas_call x0 -> x1, Pallas kernels: none -> 18.9 us  [per_device(): pl.pallas_call(functools.partial(kernel, inner, outer), out_shape=[jax.Sh...]
    reshape x8 -> x0, local copies, waits for them, and re-layouts: 8.04 us -> none  [the longest x2 3.16 us: outer_slopes(): backward.astype(jnp.bfloat16)]
    dot_general x10 -> x0, matrix products: 6.57 us -> none  [the longest x1 1.63 us: per_device(): jnp.einsum('sic,sjd->ijcd', left_block, second_operand_local, preferred_e...]
    convert_element_type x5 -> x0, local copies, waits for them, and re-layouts: 4.73 us -> none  [the longest x1 4.19 us: per_device(): products.astype(jnp.bfloat16)]
    all_to_all x1 -> x0, starting transfers between devices: 4.16 us -> none  [per_device(): lax.all_to_all(stored, 'col', split_axis=0, concat_axis=1, tiled=True)]
    unnamed x10 -> x5, local copies, waits for them, and re-layouts: 0.03 us -> 3.67 us
    all_to_all x2 -> x0, local copies, waits for them, and re-layouts: 1.52 us -> none  [per_device(): lax.all_to_all(stored, 'col', split_axis=0, concat_axis=1, tiled=True)]
  transfers between devices with their start and end apart: 1 -> 0, of which waited for: 0 -> 0; matrix products, arithmetic and copies ran while one was open for 6% -> 0% of each run, Pallas kernels for 0% -> 0%
where the time goes in v1:
time: 23.5 us; the launch traced here: 23.3 us
  Pallas kernels  18.9 us (80%)
  local copies, waits for them, and re-layouts  3.67 us (16%)
  between operations  0.65 us (3%)
    pallas_call x1, Pallas kernels, per_device(): pl.pallas_call(functools.partial(kernel, inner, outer), out_shape=[jax.Sh...  18.9 us
    unnamed x5, local copies, waits for them, and re-layouts  3.67 us

profile of v1, /device:TPU:0, one launch (start us, length us, event | category | flops | bytes accessed | tf_op | source)
XLA Modules:
  0.0 23.3 jit_solution(15243952204083695671)
XLA Ops:
  0.6 18.9 %pair_backward.1 = (f32[128,96]{1,0:T(8,128)}, f32[128,96]{1,0:T(8,128)}, bf16[96,4,256]{2,1,0:T(4,128)(2,1)}) custom-call(bf16[96,4,256]{2,1,0:T(4,128)(2,1)} %e_ref.1, bf16[32,256]{1,0:T(8,128)(2,1)} %bitcast.13, bf16[32,256]{1,0:T(8,128)(2,1)} %bitcast.14, bf16[1024,128]{1,0:T(8,128)(2,1)} %dec_ref.1, f32[1,128]{1,0:T(1,128)} %bitcast.15, ...), custom_call_target="tpu_custom_call" | custom-call | tf_op jit(solution)/shard_map/pair_backward/pallas_call | solution.py:223
  19.6 0.0 copy-start
  19.6 1.5 %copy.12 = f32[96,4,32]{0,2,1:T(8,128)} copy(f32[96,4,32]{0,2,1:T(8,128)} %bitcast.12) | data formatting | bytes 98304
  21.1 1.5 %copy.13 = f32[96,4,32]{0,2,1:T(8,128)} copy(f32[96,4,32]{0,2,1:T(8,128)} %bitcast.11) | data formatting | bytes 98304
  22.6 0.0 copy-done
  22.6 0.7 %copy.14 = bf16[96,4,256]{2,1,0:T(4,128)(2,1)} copy(bf16[96,4,256]{2,1,0:T(4,128)(2,1)S(1)} %copy-done) | data formatting | bytes 393216
Async XLA Ops:
  19.6 3.0 %copy-start = (bf16[96,4,256]{2,1,0:T(4,128)(2,1)S(1)}, bf16[96,4,256]{2,1,0:T(4,128)(2,1)}, u32[]{:S(2)}) copy-start(bf16[96,4,256]{2,1,0:T(4,128)(2,1)} %get-tuple-element.14) | copy-start | bytes 589828

commit v2 on v1

v2 whole, which is shorter than its diff:
```python
import functools

import jax
import jax.numpy as jnp
from jax import lax
from jax.experimental import pallas as pl
from jax.experimental.pallas import tpu as pltpu
from jax.sharding import PartitionSpec as P

MESH = pl.DeviceIdType.MESH
F32 = jnp.float32
BF16 = jnp.bfloat16


def dot(x, y, dims=((1,), (0,))):
    return lax.dot_general(x, y, (dims, ((), ())), preferred_element_type=F32)


NT = ((1,), (1,))
TN = ((0,), (0,))


def exchange_lanes(parts, group):
    parts = list(parts)
    width = parts[0].shape[1]
    lane = lax.broadcasted_iota(jnp.int32, parts[0].shape, 1) // group
    step = len(parts) // 2
    while step:
        high = lax.rem(lane // step, 2) == 1
        for p in range(len(parts)):
            if p // step % 2 == 0:
                x, y = parts[p], parts[p + step]
                parts[p] = jnp.where(high, pltpu.roll(y, step * group, 1), x)
                parts[p + step] = jnp.where(high, y, pltpu.roll(x, width - step * group, 1))
        step //= 2
    return parts


def place_factors(wpad, wl, wr):
    res = wpad.shape[0]
    fac = wl.shape[0]
    wpad[...] = jnp.zeros_like(wpad)
    for r in range(res):
        wpad[r, r * fac : (r + 1) * fac, :] = wl
        wpad[r, (res + r) * fac : (res + r + 1) * fac, :] = wr


def kernel(
    inner,
    outer,
    e_hbm,
    wl_hbm,
    wr_hbm,
    dec_hbm,
    bias_hbm,
    g_hbm,
    both_ref,
    e_ref,
    wl_ref,
    wr_ref,
    dec_ref,
    bias_ref,
    lbuf,
    rbuf,
    gbuf,
    fown,
    sown,
    fsend,
    ssend,
    fbuf,
    sbuf,
    wpad,
    perm,
    gf,
    mt,
    s2,
    l_ss,
    l_rs,
    r_ss,
    r_rs,
    g_ss,
    g_rs,
    f_ss,
    f_rs,
    s_ss,
    s_rs,
    in_sem,
):
    rows, res, width = e_ref.shape
    fac = wl_ref.shape[0]
    chan = dec_ref.shape[1]
    blk = res * fac
    ni = outer * res
    recip = 1.0 / rows
    me = lax.axis_index("col")
    a = lax.rem(me, inner)
    b = me // inner

    inner_peers = [lax.rem(a + k, inner) for k in range(1, inner)]
    outer_peers = [lax.rem(b + k, outer) for k in range(1, outer)]

    def inner_dev(p):
        return {"col": b * inner + p}

    def outer_dev(p):
        return {"col": p * inner + a}

    barrier = pltpu.get_barrier_semaphore()
    for p in outer_peers:
        pl.semaphore_signal(barrier, inc=1, device_id=outer_dev(p), device_id_type=MESH)
    for p in inner_peers:
        pl.semaphore_signal(barrier, inc=1, device_id=inner_dev(p), device_id_type=MESH)

    loads = []
    for k, (src, dst) in enumerate(
        [
            (wl_hbm, wl_ref),
            (wr_hbm, wr_ref),
            (e_hbm, e_ref),
            (g_hbm.at[:, pl.ds(a * res, res)], gbuf.at[a]),
            (dec_hbm, dec_ref),
            (bias_hbm, bias_ref),
        ]
    ):
        c = pltpu.make_async_copy(src, dst, in_sem.at[k])
        c.start()
        loads.append(c)

    loads[0].wait()
    loads[1].wait()
    place_factors(wpad, wl_ref[...], wr_ref[...])

    def send(src, dst, ss, rs, dev):
        c = pltpu.make_async_remote_copy(
            src_ref=src, dst_ref=dst, send_sem=ss, recv_sem=rs, device_id=dev, device_id_type=MESH
        )
        c.start()
        return c

    def arrive(buf, rs, p, dev):
        pltpu.make_async_remote_copy(
            src_ref=buf.at[p],
            dst_ref=buf.at[p],
            send_sem=rs.at[p],
            recv_sem=rs.at[p],
            device_id=dev,
            device_id_type=MESH,
        ).wait_recv()

    loads[2].wait()
    pl.semaphore_wait(barrier, inner + outer - 2)
    sends = []
    for k, p in enumerate(inner_peers):
        sends.append(
            send(
                g_hbm.at[:, pl.ds(p * res, res)], gbuf.at[a], g_ss.at[k], g_rs.at[a], inner_dev(p)
            )
        )
    acc = dot(e_ref[:, 0, :], wpad[0], NT)
    for r in range(1, res):
        acc = acc + dot(e_ref[:, r, :], wpad[r], NT)
    acc = acc.astype(BF16)
    lbuf[b] = acc[:, :blk]
    for k, p in enumerate(outer_peers):
        sends.append(send(lbuf.at[b], lbuf.at[b], l_ss.at[k], l_rs.at[b], outer_dev(p)))
    rbuf[a] = acc[:, blk:]
    for k, p in enumerate(inner_peers):
        sends.append(send(rbuf.at[a], rbuf.at[a], r_ss.at[k], r_rs.at[a], inner_dev(p)))

    out_pos = lax.broadcasted_iota(jnp.int32, perm.shape, 0)
    in_pos = lax.broadcasted_iota(jnp.int32, perm.shape, 1)
    hit = in_pos == lax.rem(out_pos, ni) * fac + out_pos // ni
    perm[...] = jnp.where(hit, 1.0, 0.0).astype(BF16)
    loads[3].wait()
    loads[4].wait()
    loads[5].wait()
    for p in inner_peers:
        arrive(gbuf, g_rs, p, inner_dev(p))
    span = inner * ni
    for q in range(inner):
        up = gbuf[q].reshape(ni, res, chan).astype(F32) * 2.0
        for r in range(res):
            gf[r * span + q * ni : r * span + (q + 1) * ni, :] = up[:, r, :]

    for p in outer_peers:
        arrive(lbuf, l_rs, p, outer_dev(p))
    left = jnp.concatenate([lbuf[q] for q in range(outer)], axis=1)
    left_p = dot(left, perm[...], NT).astype(BF16)

    for p in inner_peers:
        arrive(rbuf, r_rs, p, inner_dev(p))
    right = jnp.concatenate([rbuf[q] for q in range(inner)], axis=1)
    prod = (dot(left_p, right, TN) * recip).astype(BF16)
    for cg in range(fac // res):
        for q in range(inner):
            parts = [
                prod[c * ni : (c + 1) * ni, q * blk : (q + 1) * blk]
                for c in range(cg * res, (cg + 1) * res)
            ]
            for r, part in enumerate(exchange_lanes(parts, fac)):
                mt[r * span + q * ni : r * span + (q + 1) * ni, cg * blk : (cg + 1) * blk] = (
                    part.astype(BF16)
                )
    linear = dot(mt[...], dec_ref[...]) + bias_ref[...]
    pre = (gf[...] * jnp.maximum(linear, 0.0)).astype(BF16)
    slopes = (dot(pre, dec_ref[...], NT) * recip).astype(BF16)
    for cg in range(fac // res):
        for q in range(inner):
            parts = [
                slopes[r * span + q * ni : r * span + (q + 1) * ni, cg * blk : (cg + 1) * blk]
                for r in range(res)
            ]
            for k, part in enumerate(exchange_lanes(parts, fac)):
                c = cg * res + k
                s2[c * ni : (c + 1) * ni, q * blk : (q + 1) * blk] = part.astype(BF16)

    first_part = dot(right, s2[...], NT).astype(BF16)
    first_part = dot(first_part, perm[...])
    for q in range(outer):
        term = first_part[:, q * blk : (q + 1) * blk]
        fown[q] = term
        fsend[q] = term.astype(BF16)
    for k, p in enumerate(outer_peers):
        sends.append(send(fsend.at[p], fbuf.at[b], f_ss.at[k], f_rs.at[b], outer_dev(p)))
    second_part = dot(left_p, s2[...])
    for q in range(inner):
        term = second_part[:, q * blk : (q + 1) * blk]
        sown[q] = term
        ssend[q] = term.astype(BF16)
    for k, p in enumerate(inner_peers):
        sends.append(send(ssend.at[p], sbuf.at[a], s_ss.at[k], s_rs.at[a], inner_dev(p)))

    second = sown[a]
    for p in inner_peers:
        arrive(sbuf, s_rs, p, inner_dev(p))
        second = second + sbuf[p].astype(F32)
    both_ref[:, blk:] = second
    first = fown[b]
    for p in outer_peers:
        arrive(fbuf, f_rs, p, outer_dev(p))
        first = first + fbuf[p].astype(F32)
    both_ref[:, :blk] = first
    for c in sends:
        c.wait_send()


def finish(both_ref, wl_ref, wr_ref, first_ref, second_ref, align_ref, wpad):
    place_factors(wpad, wl_ref[...], wr_ref[...])
    both = both_ref[...]
    blk = both.shape[1] // 2
    first_ref[...] = both[:, :blk].T
    second_ref[...] = both[:, blk:].T
    both = both.astype(BF16)
    for r in range(align_ref.shape[1]):
        align_ref[:, r, :] = dot(both, wpad[r]).astype(BF16)


def per_device(
    homolog_embedding,
    left_factor_matrix,
    right_factor_matrix,
    decoder,
    pair_output_bias,
    pair_output_gradient,
):
    rows, res, width = homolog_embedding.shape
    fac = left_factor_matrix.shape[1]
    chan = decoder.shape[1]
    count = lax.axis_size("col")
    inner = max(d for d in range(1, count + 1) if count % d == 0 and d * d <= count)
    outer = count // inner
    blk = res * fac
    ni = outer * res
    dma = pltpu.SemaphoreType.DMA
    vmem = pl.BlockSpec(memory_space=pltpu.VMEM)
    left_t = left_factor_matrix.T
    right_t = right_factor_matrix.T
    both = pl.pallas_call(
        functools.partial(kernel, inner, outer),
        out_shape=jax.ShapeDtypeStruct((rows, 2 * blk), F32),
        in_specs=[pl.BlockSpec(memory_space=pl.ANY)] * 6,
        out_specs=vmem,
        scratch_shapes=[
            pltpu.VMEM((rows, res, width), BF16),
            pltpu.VMEM((fac, width), BF16),
            pltpu.VMEM((fac, width), BF16),
            pltpu.VMEM(decoder.shape, BF16),
            pltpu.VMEM((1, chan), F32),
            pltpu.VMEM((outer, rows, blk), BF16),
            pltpu.VMEM((inner, rows, blk), BF16),
            pltpu.VMEM((inner, outer, res, res, chan), BF16),
            pltpu.VMEM((outer, rows, blk), F32),
            pltpu.VMEM((inner, rows, blk), F32),
            pltpu.VMEM((outer, rows, blk), BF16),
            pltpu.VMEM((inner, rows, blk), BF16),
            pltpu.VMEM((outer, rows, blk), BF16),
            pltpu.VMEM((inner, rows, blk), BF16),
            pltpu.VMEM((res, 2 * blk, width), BF16),
            pltpu.VMEM((fac * ni, fac * ni), BF16),
            pltpu.VMEM((res * inner * ni, chan), F32),
            pltpu.VMEM((res * inner * ni, fac * fac), BF16),
            pltpu.VMEM((fac * ni, inner * blk), BF16),
            dma((outer,)),
            dma((outer,)),
            dma((inner,)),
            dma((inner,)),
            dma((inner,)),
            dma((inner,)),
            dma((outer,)),
            dma((outer,)),
            dma((inner,)),
            dma((inner,)),
            dma((6,)),
        ],
        compiler_params=pltpu.CompilerParams(collective_id=0, has_side_effects=True),
        name="pair_backward",
    )(
        homolog_embedding,
        left_t,
        right_t,
        decoder,
        pair_output_bias.reshape(1, chan),
        pair_output_gradient.reshape(outer, inner * res, res, chan),
    )
    first, second, align = pl.pallas_call(
        finish,
        out_shape=[
            jax.ShapeDtypeStruct((blk, rows), F32),
            jax.ShapeDtypeStruct((blk, rows), F32),
            jax.ShapeDtypeStruct((rows, res, width), BF16),
        ],
        in_specs=[vmem] * 3,
        out_specs=[vmem] * 3,
        scratch_shapes=[pltpu.VMEM((res, 2 * blk, width), BF16)],
        name="finish",
    )(both, left_t, right_t)
    first = first.reshape(res, fac, rows).transpose(2, 0, 1)
    second = second.reshape(res, fac, rows).transpose(2, 0, 1)
    return first, second, align


def solution(mesh):
    placed = (P("group", "col", None), P(), P(), P(), P(), P("group", "col", None))
    return jax.shard_map(
        per_device,
        mesh=mesh,
        in_specs=placed,
        out_specs=(P("group", "col", None), P("group", "col", None), P("group", "col", None)),
        check_vma=False,
    )
```

time: 23.5 us -> 19.6 us (0.83)
  local copies, waits for them, and re-layouts: 3.67 us -> 0 us
    unnamed x5 -> x0, local copies, waits for them, and re-layouts: 3.67 us -> none
    pallas_call x1 -> x2, Pallas kernels: 18.9 us -> 18.8 us  [the longest x1 16.8 us: per_device(): pl.pallas_call(functools.partial(kernel, inner, outer), out_shape=jax.Sha...]
where the time goes in v2:
time: 19.6 us; the launch traced here: 19.4 us
  Pallas kernels  18.8 us (96%)
  between operations  0.64 us (3%)
    pallas_call x1, Pallas kernels, per_device(): pl.pallas_call(functools.partial(kernel, inner, outer), out_shape=jax.Sha...  16.8 us
    pallas_call x1, Pallas kernels, per_device(): pl.pallas_call(finish, out_shape=[jax.ShapeDtypeStruct((blk, rows), F32),...  1.99 us

profile of v2, /device:TPU:0, one launch (start us, length us, event | category | flops | bytes accessed | tf_op | source)
XLA Modules:
  0.0 19.4 jit_solution(404980777213280153)
XLA Ops:
  0.6 16.8 %pair_backward.1.both_ref = f32[96,256]{1,0:T(8,128)} custom-call(bf16[96,4,256]{2,1,0:T(4,128)(2,1)} %e_hbm.1, bf16[32,256]{1,0:T(8,128)(2,1)} %bitcast.11, bf16[32,256]{1,0:T(8,128)(2,1)} %bitcast.13, bf16[1024,128]{1,0:T(8,128)(2,1)} %dec_hbm.1, f32[1,128]{1,0:T(1,128)} %bitcast.15, bf16[4,16,4,128]{3,2,1,0:T(4,128)(2,1)} %bitcast.10), custom_call_target="tpu_custom_call" | custom-call | tf_op jit(solution)/shard_map/pair_backward/pallas_call | solution.py:278
  17.4 2.0 %finish.1 = (f32[128,96]{1,0:T(8,128)}, f32[128,96]{1,0:T(8,128)}, bf16[96,4,256]{2,1,0:T(4,128)(2,1)}) custom-call(f32[96,256]{1,0:T(8,128)} %pair_backward.1.both_ref, bf16[32,256]{1,0:T(8,128)(2,1)} %bitcast.12, bf16[32,256]{1,0:T(8,128)(2,1)} %bitcast.14), custom_call_target="tpu_custom_call" | custom-call | tf_op jit(solution)/shard_map/finish/pallas_call | solution.py:325

commit v3 on v2

--- a/solution.py
+++ b/solution.py
@@ -18,22 +18,6 @@
 
 NT = ((1,), (1,))
 TN = ((0,), (0,))
-
-
-def exchange_lanes(parts, group):
-    parts = list(parts)
-    width = parts[0].shape[1]
-    lane = lax.broadcasted_iota(jnp.int32, parts[0].shape, 1) // group
-    step = len(parts) // 2
-    while step:
-        high = lax.rem(lane // step, 2) == 1
-        for p in range(len(parts)):
-            if p // step % 2 == 0:
-                x, y = parts[p], parts[p + step]
-                parts[p] = jnp.where(high, pltpu.roll(y, step * group, 1), x)
-                parts[p + step] = jnp.where(high, y, pltpu.roll(x, width - step * group, 1))
-        step //= 2
-    return parts
 
 
 def place_factors(wpad, wl, wr):
@@ -69,8 +53,11 @@
     ssend,
     fbuf,
     sbuf,
-    wpad,
+    wtile,
+    mask,
+    pick,
     perm,
+    swap,
     gf,
     mt,
     s2,
@@ -97,7 +84,12 @@
     b = me // inner
 
     inner_peers = [lax.rem(a + k, inner) for k in range(1, inner)]
-    outer_peers = [lax.rem(b + k, outer) for k in range(1, outer)]
+    outer_peers = []
+    for k in range(outer - 1):
+        low = outer - 1 - k
+        low = jnp.where(low > b, low, low - 1)
+        high = jnp.where(k < b, k, k + 1)
+        outer_peers.append(jnp.where(2 * b < outer, low, high))
 
     def inner_dev(p):
         return {"col": b * inner + p}
@@ -126,9 +118,18 @@
         c.start()
         loads.append(c)
 
+    row_pos = lax.broadcasted_iota(jnp.int32, mask.shape, 0)
+    lane_pos = lax.broadcasted_iota(jnp.int32, mask.shape, 1)
+    mask[...] = jnp.where(lax.rem(row_pos, res) == lax.rem(lane_pos // fac, res), 1.0, 0.0)
+    row_pos = lax.broadcasted_iota(jnp.int32, pick.shape, 0)
+    lane_pos = lax.broadcasted_iota(jnp.int32, pick.shape, 1)
+    pick[...] = jnp.where(lane_pos // res == row_pos, 1.0, 0.0).astype(BF16)
+
     loads[0].wait()
     loads[1].wait()
-    place_factors(wpad, wl_ref[...], wr_ref[...])
+    for r in range(res):
+        wtile[r * fac : (r + 1) * fac, :] = wl_ref[...]
+        wtile[(res + r) * fac : (res + r + 1) * fac, :] = wr_ref[...]
 
     def send(src, dst, ss, rs, dev):
         c = pltpu.make_async_remote_copy(
@@ -156,10 +157,9 @@
                 g_hbm.at[:, pl.ds(p * res, res)], gbuf.at[a], g_ss.at[k], g_rs.at[a], inner_dev(p)
             )
         )
-    acc = dot(e_ref[:, 0, :], wpad[0], NT)
-    for r in range(1, res):
-        acc = acc + dot(e_ref[:, r, :], wpad[r], NT)
-    acc = acc.astype(BF16)
+    flat = dot(e_ref[...].reshape(rows * res, width), wtile[...], NT)
+    flat = jnp.where(mask[...] > 0.0, flat, 0.0)
+    acc = dot(pick[...], flat.astype(BF16)).astype(BF16)
     lbuf[b] = acc[:, :blk]
     for k, p in enumerate(outer_peers):
         sends.append(send(lbuf.at[b], lbuf.at[b], l_ss.at[k], l_rs.at[b], outer_dev(p)))
@@ -171,6 +171,14 @@
     in_pos = lax.broadcasted_iota(jnp.int32, perm.shape, 1)
     hit = in_pos == lax.rem(out_pos, ni) * fac + out_pos // ni
     perm[...] = jnp.where(hit, 1.0, 0.0).astype(BF16)
+    out_pos = lax.broadcasted_iota(jnp.int32, swap.shape, 0)
+    in_pos = lax.broadcasted_iota(jnp.int32, swap.shape, 1)
+    hit = (
+        (out_pos // blk == lax.rem(in_pos // fac, res))
+        & (in_pos // blk == lax.rem(out_pos // fac, res))
+        & (lax.rem(out_pos, fac) == lax.rem(in_pos, fac))
+    )
+    swap[...] = jnp.where(hit, 1.0, 0.0).astype(BF16)
     loads[3].wait()
     loads[4].wait()
     loads[5].wait()
@@ -191,28 +199,49 @@
         arrive(rbuf, r_rs, p, inner_dev(p))
     right = jnp.concatenate([rbuf[q] for q in range(inner)], axis=1)
     prod = (dot(left_p, right, TN) * recip).astype(BF16)
-    for cg in range(fac // res):
-        for q in range(inner):
-            parts = [
-                prod[c * ni : (c + 1) * ni, q * blk : (q + 1) * blk]
-                for c in range(cg * res, (cg + 1) * res)
+    groups = [(cg, q) for cg in range(fac // res) for q in range(inner)]
+    mixed = jnp.concatenate(
+        [
+            jnp.concatenate(
+                [
+                    prod[(cg * res + k) * ni : (cg * res + k + 1) * ni, q * blk : (q + 1) * blk]
+                    for cg, q in groups
+                ],
+                axis=0,
+            )
+            for k in range(res)
+        ],
+        axis=1,
+    )
+    mixed = dot(mixed, swap[...]).astype(BF16)
+    for n, (cg, q) in enumerate(groups):
+        for r in range(res):
+            mt[r * span + q * ni : r * span + (q + 1) * ni, cg * blk : (cg + 1) * blk] = mixed[
+                n * ni : (n + 1) * ni, r * blk : (r + 1) * blk
             ]
-            for r, part in enumerate(exchange_lanes(parts, fac)):
-                mt[r * span + q * ni : r * span + (q + 1) * ni, cg * blk : (cg + 1) * blk] = (
-                    part.astype(BF16)
-                )
     linear = dot(mt[...], dec_ref[...]) + bias_ref[...]
     pre = (gf[...] * jnp.maximum(linear, 0.0)).astype(BF16)
     slopes = (dot(pre, dec_ref[...], NT) * recip).astype(BF16)
-    for cg in range(fac // res):
-        for q in range(inner):
-            parts = [
-                slopes[r * span + q * ni : r * span + (q + 1) * ni, cg * blk : (cg + 1) * blk]
-                for r in range(res)
+    mixed = jnp.concatenate(
+        [
+            jnp.concatenate(
+                [
+                    slopes[r * span + q * ni : r * span + (q + 1) * ni, cg * blk : (cg + 1) * blk]
+                    for cg, q in groups
+                ],
+                axis=0,
+            )
+            for r in range(res)
+        ],
+        axis=1,
+    )
+    mixed = dot(mixed, swap[...]).astype(BF16)
+    for n, (cg, q) in enumerate(groups):
+        for k in range(res):
+            c = cg * res + k
+            s2[c * ni : (c + 1) * ni, q * blk : (q + 1) * blk] = mixed[
+                n * ni : (n + 1) * ni, k * blk : (k + 1) * blk
             ]
-            for k, part in enumerate(exchange_lanes(parts, fac)):
-                c = cg * res + k
-                s2[c * ni : (c + 1) * ni, q * blk : (q + 1) * blk] = part.astype(BF16)
 
     first_part = dot(right, s2[...], NT).astype(BF16)
     first_part = dot(first_part, perm[...])
@@ -278,7 +307,7 @@
     both = pl.pallas_call(
         functools.partial(kernel, inner, outer),
         out_shape=jax.ShapeDtypeStruct((rows, 2 * blk), F32),
-        in_specs=[pl.BlockSpec(memory_space=pl.ANY)] * 6,
+        in_specs=[pl.BlockSpec(memory_space=pltpu.HBM)] * 6,
         out_specs=vmem,
         scratch_shapes=[
             pltpu.VMEM((rows, res, width), BF16),
@@ -295,8 +324,11 @@
             pltpu.VMEM((inner, rows, blk), BF16),
             pltpu.VMEM((outer, rows, blk), BF16),
             pltpu.VMEM((inner, rows, blk), BF16),
-            pltpu.VMEM((res, 2 * blk, width), BF16),
+            pltpu.VMEM((2 * blk, width), BF16),
+            pltpu.VMEM((rows * res, 2 * blk), F32),
+            pltpu.VMEM((rows, rows * res), BF16),
             pltpu.VMEM((fac * ni, fac * ni), BF16),
+            pltpu.VMEM((res * blk, res * blk), BF16),
             pltpu.VMEM((res * inner * ni, chan), F32),
             pltpu.VMEM((res * inner * ni, fac * fac), BF16),
             pltpu.VMEM((fac * ni, inner * blk), BF16),
@@ -312,15 +344,20 @@
             dma((inner,)),
             dma((6,)),
         ],
-        compiler_params=pltpu.CompilerParams(collective_id=0, has_side_effects=True),
+        compiler_params=pltpu.CompilerParams(collective_id=0, has_side_effects=True, vmem_limit_bytes=24 * 1024 * 1024),
         name="pair_backward",
     )(
-        homolog_embedding,
-        left_t,
-        right_t,
-        decoder,
-        pair_output_bias.reshape(1, chan),
-        pair_output_gradient.reshape(outer, inner * res, res, chan),
+        *[
+            pltpu.with_memory_space_constraint(x, pltpu.HBM)
+            for x in (
+                homolog_embedding,
+                left_t,
+                right_t,
+                decoder,
+                pair_output_bias.reshape(1, chan),
+                pair_output_gradient.reshape(outer, inner * res, res, chan),
+            )
+        ]
     )
     first, second, align = pl.pallas_call(
         finish,
@@ -332,6 +369,7 @@
         in_specs=[vmem] * 3,
         out_specs=[vmem] * 3,
         scratch_shapes=[pltpu.VMEM((res, 2 * blk, width), BF16)],
+        compiler_params=pltpu.CompilerParams(vmem_limit_bytes=16 * 1024 * 1024),
         name="finish",
     )(both, left_t, right_t)
     first = first.reshape(res, fac, rows).transpose(2, 0, 1)

time: 19.6 us -> 17.3 us (0.88)
  Pallas kernels: 18.8 us -> 16.5 us
    pallas_call x1, Pallas kernels: 16.8 us -> 15.4 us  [per_device(): pl.pallas_call(functools.partial(kernel, inner, outer), out_shape=jax.Sha...]
    pallas_call x1, Pallas kernels: 1.99 us -> 1.08 us  [per_device(): pl.pallas_call(finish, out_shape=[jax.ShapeDtypeStruct((blk, rows), F32),...]
where the time goes in v3:
time: 17.3 us; the launch traced here: 17.2 us
  Pallas kernels  16.5 us (95%)
  between operations  0.67 us (4%)
    pallas_call x1, Pallas kernels, per_device(): pl.pallas_call(functools.partial(kernel, inner, outer), out_shape=jax.Sha...  15.4 us
    pallas_call x1, Pallas kernels, per_device(): pl.pallas_call(finish, out_shape=[jax.ShapeDtypeStruct((blk, rows), F32),...  1.08 us

profile of v3, /device:TPU:0, one launch (start us, length us, event | category | flops | bytes accessed | tf_op | source)
XLA Modules:
  0.0 17.2 jit_solution(11047030168505888266)
XLA Ops:
  0.6 0.0 copy-start
  0.6 0.0 copy-start.1
  0.7 15.4 %pair_backward.1.both_ref = f32[96,256]{1,0:T(8,128)S(1)} custom-call(bf16[96,4,256]{2,1,0:T(4,128)(2,1)} %e_hbm.1, bf16[32,256]{1,0:T(8,128)(2,1)} %bitcast.10, bf16[32,256]{1,0:T(8,128)(2,1)} %bitcast.12, bf16[1024,128]{1,0:T(8,128)(2,1)} %dec_hbm.1, f32[1,128]{1,0:T(1,128)} %bitcast.15, bf16[4,16,4,128]{3,2,1,0:T(4,128)(2,1)} %bitcast.14), custom_call_target="tpu_custom_call" | custom-call | tf_op jit(solution)/shard_map/pair_backward/pallas_call | solution.py:307
  16.1 0.0 copy-done
  16.1 0.0 copy-done.1
  16.1 1.1 %finish.1 = (f32[128,96]{1,0:T(8,128)}, f32[128,96]{1,0:T(8,128)}, bf16[96,4,256]{2,1,0:T(4,128)(2,1)}) custom-call(f32[96,256]{1,0:T(8,128)S(1)} %pair_backward.1.both_ref, bf16[32,256]{1,0:T(8,128)(2,1)S(1)} %bitcast.11, bf16[32,256]{1,0:T(8,128)(2,1)S(1)} %bitcast.13), custom_call_target="tpu_custom_call" | custom-call | tf_op jit(solution)/shard_map/finish/pallas_call | solution.py:362
Async XLA Ops:
  0.6 15.4 %copy-start = (bf16[256,32]{0,1:T(8,128)(2,1)S(1)}, bf16[256,32]{0,1:T(8,128)(2,1)}, u32[]{:S(2)}) copy-start(bf16[256,32]{0,1:T(8,128)(2,1)} %param.7) | copy-start | bytes 49156
  0.6 15.4 %copy-start.1 = (bf16[256,32]{0,1:T(8,128)(2,1)S(1)}, bf16[256,32]{0,1:T(8,128)(2,1)}, u32[]{:S(2)}) copy-start(bf16[256,32]{0,1:T(8,128)(2,1)} %param.8) | copy-start | bytes 49156

commit v4 on v3

--- a/solution.py
+++ b/solution.py
@@ -149,24 +149,24 @@
         ).wait_recv()
 
     loads[2].wait()
+    sends = []
+    flat = dot(e_ref[...].reshape(rows * res, width), wtile[...], NT)
+    flat = jnp.where(mask[...] > 0.0, flat, 0.0)
+    acc = dot(pick[...], flat.astype(BF16)).astype(BF16)
+    lbuf[b] = acc[:, :blk]
     pl.semaphore_wait(barrier, inner + outer - 2)
-    sends = []
+    for k, p in enumerate(outer_peers):
+        sends.append(send(lbuf.at[b], lbuf.at[b], l_ss.at[k], l_rs.at[b], outer_dev(p)))
+    rbuf[a] = acc[:, blk:]
+    for k, p in enumerate(inner_peers):
+        sends.append(send(rbuf.at[a], rbuf.at[a], r_ss.at[k], r_rs.at[a], inner_dev(p)))
+
     for k, p in enumerate(inner_peers):
         sends.append(
             send(
                 g_hbm.at[:, pl.ds(p * res, res)], gbuf.at[a], g_ss.at[k], g_rs.at[a], inner_dev(p)
             )
         )
-    flat = dot(e_ref[...].reshape(rows * res, width), wtile[...], NT)
-    flat = jnp.where(mask[...] > 0.0, flat, 0.0)
-    acc = dot(pick[...], flat.astype(BF16)).astype(BF16)
-    lbuf[b] = acc[:, :blk]
-    for k, p in enumerate(outer_peers):
-        sends.append(send(lbuf.at[b], lbuf.at[b], l_ss.at[k], l_rs.at[b], outer_dev(p)))
-    rbuf[a] = acc[:, blk:]
-    for k, p in enumerate(inner_peers):
-        sends.append(send(rbuf.at[a], rbuf.at[a], r_ss.at[k], r_rs.at[a], inner_dev(p)))
-
     out_pos = lax.broadcasted_iota(jnp.int32, perm.shape, 0)
     in_pos = lax.broadcasted_iota(jnp.int32, perm.shape, 1)
     hit = in_pos == lax.rem(out_pos, ni) * fac + out_pos // ni

time: 17.3 us -> 17 us (0.983)
  Pallas kernels: 16.5 us -> 16.2 us
    pallas_call x1, Pallas kernels: 15.4 us -> 15.1 us  [per_device(): pl.pallas_call(functools.partial(kernel, inner, outer), out_shape=jax.Sha...]
where the time goes in v4:
time: 17 us; the launch traced here: 16.8 us
  Pallas kernels  16.2 us (95%)
  between operations  0.67 us (4%)
    pallas_call x1, Pallas kernels, per_device(): pl.pallas_call(functools.partial(kernel, inner, outer), out_shape=jax.Sha...  15.1 us
    pallas_call x1, Pallas kernels, per_device(): pl.pallas_call(finish, out_shape=[jax.ShapeDtypeStruct((blk, rows), F32),...  1.08 us

profile of v4, /device:TPU:0, one launch (start us, length us, event | category | flops | bytes accessed | tf_op | source)
XLA Modules:
  0.0 16.8 jit_solution(11987234895968917112)
XLA Ops:
  0.6 0.0 copy-start
  0.6 0.0 copy-start.1
  0.7 15.1 %pair_backward.1.both_ref = f32[96,256]{1,0:T(8,128)S(1)} custom-call(bf16[96,4,256]{2,1,0:T(4,128)(2,1)} %e_hbm.1, bf16[32,256]{1,0:T(8,128)(2,1)} %bitcast.10, bf16[32,256]{1,0:T(8,128)(2,1)} %bitcast.12, bf16[1024,128]{1,0:T(8,128)(2,1)} %dec_hbm.1, f32[1,128]{1,0:T(1,128)} %bitcast.15, bf16[4,16,4,128]{3,2,1,0:T(4,128)(2,1)} %bitcast.14), custom_call_target="tpu_custom_call" | custom-call | tf_op jit(solution)/shard_map/pair_backward/pallas_call | solution.py:307
  15.7 0.0 copy-done
  15.8 0.0 copy-done.1
  15.8 1.1 %finish.1 = (f32[128,96]{1,0:T(8,128)}, f32[128,96]{1,0:T(8,128)}, bf16[96,4,256]{2,1,0:T(4,128)(2,1)}) custom-call(f32[96,256]{1,0:T(8,128)S(1)} %pair_backward.1.both_ref, bf16[32,256]{1,0:T(8,128)(2,1)S(1)} %bitcast.11, bf16[32,256]{1,0:T(8,128)(2,1)S(1)} %bitcast.13), custom_call_target="tpu_custom_call" | custom-call | tf_op jit(solution)/shard_map/finish/pallas_call | solution.py:362
Async XLA Ops:
  0.6 15.1 %copy-start = (bf16[256,32]{0,1:T(8,128)(2,1)S(1)}, bf16[256,32]{0,1:T(8,128)(2,1)}, u32[]{:S(2)}) copy-start(bf16[256,32]{0,1:T(8,128)(2,1)} %param.7) | copy-start | bytes 49156
  0.6 15.1 %copy-start.1 = (bf16[256,32]{0,1:T(8,128)(2,1)S(1)}, bf16[256,32]{0,1:T(8,128)(2,1)}, u32[]{:S(2)}) copy-start(bf16[256,32]{0,1:T(8,128)(2,1)} %param.8) | copy-start | bytes 49156
